TPU v7x, 512 devices: a whole 4x8x8 slice. The times are simulated.
512 devices in a mesh: section: 16 (over y, z_hi), dp: 32 (over z_lo, x, core).
Axes of the slice: x: 4, y: 8, z: 8 (z_hi: 2, z_lo: 4; z = z_hi * 4 + z_lo), core: 2. Of those that a mesh axis runs over, the one named last changes fastest.
Arguments:
- section_input: bfloat16 [6, 768, 3072], P(None, 'dp'), may hold values from -6 to 6
- loss_grad: bfloat16 [6, 768, 3072], P(None, 'dp'), may hold values from -6 to 6
- norm_gain: float32 [16, 3072], P('section'), may hold values from 0.1 to 1.9
- channel_order: int32 [16, 3072], P('section'), may hold values from 0 to 3071, each once within a row
- right_factor: bfloat16 [16, 3072, 768], P('section', 'dp'), may hold values from -0.15625 to 0.15625
- left_factor: bfloat16 [16, 3072, 768], P('section', 'dp'), may hold values from -0.15625 to 0.15625
Outputs:
- section_output: bfloat16 [16, 6, 768, 3072], P('section', None, 'dp')
- left_grad: float32 [16, 768, 768], P('section', 'dp')
Inputs may be any that keep to these rules, and one draw needn't show every extreme that they name: `channel_order`: each layer's row is a permutation of the 3072 channels.
All inputs are finite; a program needn't handle non-finite values.
Results may differ from a plain program's by a relative error of at most 0.03.
Values may be sent and summed in bfloat16 or wider, within the bound.
A program may use at most 64 MiB of HBM per device.

v0:
```python
import jax
import jax.numpy as jnp
from jax import lax
from jax.sharding import PartitionSpec as P

epsilon = 1e-05


def shifted(array, axis, by):
    peers = lax.axis_size(axis)
    pairs = [(i, i + by) for i in range(peers) if 0 <= i + by < peers]
    return lax.ppermute(array, axis, pairs)


def block_apply(values, factor):
    row_count = values.shape[0]
    block_size = factor.shape[1]
    block_count = factor.shape[0] // block_size
    result = jnp.einsum(
        "rnk,nkj->rnj",
        values.reshape(row_count, block_count, block_size),
        factor.reshape(block_count, block_size, block_size),
        preferred_element_type=jnp.float32,
    )
    return result.reshape(row_count, block_count * block_size)


def block_transposed(values, factor):
    row_count = values.shape[0]
    block_size = factor.shape[1]
    block_count = factor.shape[0] // block_size
    result = jnp.einsum(
        "rnj,nkj->rnk",
        values.reshape(row_count, block_count, block_size),
        factor.reshape(block_count, block_size, block_size),
        preferred_element_type=jnp.float32,
    )
    return result.reshape(row_count, block_count * block_size)


def inverse_norm(inputs):
    wide_in = inputs.astype(jnp.float32)
    return (wide_in, lax.rsqrt(jnp.mean(wide_in * wide_in, axis=-1, keepdims=True) + epsilon))


def layer_forward(inputs, gain_row, shuffle, right_full, left_full):
    wide_in, inverse_rms = inverse_norm(inputs)
    normed = (wide_in * inverse_rms * gain_row).astype(jnp.bfloat16)
    mixed = block_apply(normed, right_full).astype(jnp.bfloat16)
    permuted = jnp.take(mixed, shuffle, axis=1)
    output = (wide_in + block_apply(permuted, left_full)).astype(jnp.bfloat16)
    return (output, permuted)


def layer_backward(inputs, upstream, gain_row, inverse, right_full, left_full):
    wide_in, inverse_rms = inverse_norm(inputs)
    through = block_transposed(upstream, left_full).astype(jnp.bfloat16)
    before = jnp.take(through, inverse, axis=1)
    scaled = block_transposed(before, right_full) * gain_row
    cubed = inverse_rms * inverse_rms * inverse_rms
    grad_input = (
        upstream.astype(jnp.float32)
        + inverse_rms * scaled
        - wide_in * cubed * jnp.mean(scaled * wide_in, axis=-1, keepdims=True)
    )
    return grad_input.astype(jnp.bfloat16)


def store_slot(buffer, batch_slot, is_valid, new_value):
    old_value = lax.dynamic_index_in_dim(buffer, batch_slot, 0, keepdims=False)
    return lax.dynamic_update_index_in_dim(
        buffer, jnp.where(is_valid, new_value, old_value), batch_slot, 0
    )


def per_device(section_input, loss_grad, norm_gain, channel_order, right_factor, left_factor):
    sections = lax.axis_size("section")
    section_index = lax.axis_index("section")
    micro_count, row_count, channels = section_input.shape
    block_size = right_factor.shape[2]
    right_full, left_full = (
        lax.all_gather(right_factor[0], "dp", axis=0, tiled=True),
        lax.all_gather(left_factor[0], "dp", axis=0, tiled=True),
    )
    gain_row = norm_gain[0]
    shuffle = channel_order[0]
    inverse = (
        jnp.zeros((channels,), jnp.int32).at[shuffle].set(jnp.arange(channels, dtype=jnp.int32))
    )
    empty_buf = jnp.zeros((micro_count, row_count, channels), jnp.bfloat16)
    empty_head = jnp.zeros((micro_count, row_count, block_size), jnp.bfloat16)
    empty_rows = jnp.zeros((row_count, channels), jnp.bfloat16)
    is_first = section_index == 0
    is_last = section_index == sections - 1

    def run_forward(inputs):
        output, permuted = layer_forward(inputs, gain_row, shuffle, right_full, left_full)
        return (output, permuted[:, :block_size])

    def skip_forward(inputs):
        return (jnp.zeros_like(inputs), jnp.zeros((row_count, block_size), jnp.bfloat16))

    def run_backward(operands):
        return layer_backward(operands[0], operands[1], gain_row, inverse, right_full, left_full)

    def skip_backward(operands):
        return jnp.zeros_like(operands[1])

    def forward_part(forward_state, step_num):
        incoming, saved_in, saved_permuted, outputs = forward_state
        batch_pos = step_num - section_index
        is_valid = (batch_pos >= 0) & (batch_pos < micro_count)
        batch_slot = jnp.clip(batch_pos, 0, micro_count - 1)
        inputs = jnp.where(
            is_first,
            lax.dynamic_index_in_dim(section_input, batch_slot, 0, keepdims=False),
            incoming,
        )
        output, permuted_head = lax.cond(is_valid, run_forward, skip_forward, inputs)
        saved_in = store_slot(saved_in, batch_slot, is_valid, inputs)
        saved_permuted = store_slot(saved_permuted, batch_slot, is_valid, permuted_head)
        outputs = store_slot(outputs, batch_slot, is_valid, output)
        passed = shifted(output, "section", 1)
        return (passed, saved_in, saved_permuted, outputs)

    def backward_part(backward_state, saved_in, step_num, lag_steps):
        incoming, saved_upstream = backward_state
        batch_pos = step_num - lag_steps + section_index
        is_valid = (batch_pos >= 0) & (batch_pos < micro_count)
        batch_slot = jnp.clip(batch_pos, 0, micro_count - 1)
        upstream = jnp.where(
            is_last, lax.dynamic_index_in_dim(loss_grad, batch_slot, 0, keepdims=False), incoming
        )
        inputs = lax.dynamic_index_in_dim(saved_in, batch_slot, 0, keepdims=False)
        grad_input = lax.cond(is_valid, run_backward, skip_backward, (inputs, upstream))
        saved_upstream = store_slot(saved_upstream, batch_slot, is_valid, upstream[:, :block_size])
        passed = shifted(grad_input, "section", -1)
        return (passed, saved_upstream)

    forward_init = (empty_rows, empty_buf, empty_head, empty_buf)
    backward_init = (empty_rows, empty_head)

    def forward_step(forward_state, step_num):
        return (forward_part(forward_state, step_num), None)

    forward_state, ignored = lax.scan(
        forward_step, forward_init, jnp.arange(sections + micro_count - 1, dtype=jnp.int32)
    )

    def backward_step(backward_state, step_num):
        return (backward_part(backward_state, forward_state[1], step_num, sections - 1), None)

    backward_state, ignored = lax.scan(
        backward_step, backward_init, jnp.arange(sections + micro_count - 1, dtype=jnp.int32)
    )
    row_total = micro_count * row_count
    left_rows = forward_state[2].reshape(row_total, block_size)
    right_rows = backward_state[1].reshape(row_total, block_size)
    left_term = lax.dot_general(
        left_rows, right_rows, (((0,), (0,)), ((), ())), preferred_element_type=jnp.float32
    )
    left_term = left_term.astype(jnp.bfloat16)
    left_total = lax.psum(left_term, "dp").astype(jnp.float32)
    share_rows = block_size // lax.axis_size("dp")
    first_row = lax.axis_index("dp") * share_rows
    left_shard = lax.dynamic_slice_in_dim(left_total, first_row, share_rows, 0)
    return (forward_state[3][None], left_shard[None])


def solution(mesh):
    in_specs = (
        P(None, "dp", None),
        P(None, "dp", None),
        P("section", None),
        P("section", None),
        P("section", "dp", None),
        P("section", "dp", None),
    )
    out_specs = (P("section", None, "dp", None), P("section", "dp", None))
    return jax.shard_map(
        per_device, mesh=mesh, in_specs=in_specs, out_specs=out_specs, check_vma=False
    )
```

profile of v0, /device:TPU:8, one launch (start us, length us, event | category | flops | bytes accessed | tf_op | source)
XLA Modules:
  0.0 1806.3 jit_solution(8007107845714510100)
XLA Ops:
  21.3 59.8 %all-gather.5.cloned.1.call-done = bf16[1,3072,768]{2,1,0:T(8,128)(2,1)} async-done(((bf16[1,96,768]{2,1,0:T(8,128)(2,1)}), bf16[1,3072,768]{2,1,0:T(8,128)(2,1)}) %all-gather.5.cloned.1.call-update) | async-done | bytes 4718608 | tf_op jit(solution)/shard_map/all_gather | solution.py:82
  81.0 67.5 %all-gather.7.cloned.1.call-done = bf16[1,3072,768]{2,1,0:T(8,128)(2,1)} async-done(((bf16[1,96,768]{2,1,0:T(8,128)(2,1)}), bf16[1,3072,768]{2,1,0:T(8,128)(2,1)}) %all-gather.7.cloned.1.call-update) | async-done | bytes 4718608 | tf_op jit(solution)/shard_map/all_gather | solution.py:83
  150.8 549.9 %while.30 = (s32[]{:T(128)}, bf16[24,3072]{1,0:T(8,128)(2,1)S(1)}, bf16[6,24,3072]{2,1,0:T(8,128)(2,1)S(1)}, bf16[6,24,768]{1,2,0:T(8,128)(2,1)}, bf16[6,24,3072...) while((s32[]{:T(128)}, bf16[24,3072]{1,0:T(8,128)(2,1)S(1)}, ...), condition=%wide.region_4.6_spmd, body=%wide.region_0.5_spmd.sunk | while | flops 227721248 | bytes 15824611 | solution.py:146
  179.9 32.0 %collective-permute-done = bf16[24,3072]{1,0:T(8,128)(2,1)S(1)} collective-permute-done((bf16[24,3072]{1,0:T(8,128)(2,1)S(1)}, bf16[24,3072]{1,0:T(8,128)(2,1)S(1)}, u32[]{:S(2)}, u32[]{:S(2)}) %collective-permute-start) | collective-permute-done | bytes 147488 | tf_op jit(solution)/shard_map/while/body/eval_jaxpr/ppermute | solution.py:12
  214.2 19.4 %conditional.4 = (bf16[24,3072]{1,0:T(8,128)(2,1)S(1)}, bf16[24,768]{0,1:T(8,128)(2,1)S(1)}) conditional(s32[]{:T(128)} %convert_element_type.97, () %tuple.71, (bf16[24,3072]{1,0:T(8,128)(2,1)S(1)}, f32[1,3072]{1,0:T(1,128)S(1)}, bf16[3072,768]{1,0:T(8,128)(2,1)}, s32[3072]{0:T(1024)S(1)}, bf16[3072,768]{1,0:T(8,128)(2,1)}) %tuple.72), branch_computations={%region_1.1_spmd, %region_2.4_spmd} | conditional | flops 227481632 | bytes 13120912 | solution.py:119
  249.5 19.4 %conditional.4 = (bf16[24,3072]{1,0:T(8,128)(2,1)S(1)}, bf16[24,768]{0,1:T(8,128)(2,1)S(1)}) conditional(s32[]{:T(128)} %convert_element_type.97, () %tuple.71, (bf16[24,3072]{1,0:T(8,128)(2,1)S(1)}, f32[1,3072]{1,0:T(1,128)S(1)}, bf16[3072,768]{1,0:T(8,128)(2,1)}, s32[3072]{0:T(1024)S(1)}, bf16[3072,768]{1,0:T(8,128)(2,1)}) %tuple.72), branch_computations={%region_1.1_spmd, %region_2.4_spmd} | conditional | flops 227481632 | bytes 13120912 | solution.py:119
  284.7 19.4 %conditional.4 = (bf16[24,3072]{1,0:T(8,128)(2,1)S(1)}, bf16[24,768]{0,1:T(8,128)(2,1)S(1)}) conditional(s32[]{:T(128)} %convert_element_type.97, () %tuple.71, (bf16[24,3072]{1,0:T(8,128)(2,1)S(1)}, f32[1,3072]{1,0:T(1,128)S(1)}, bf16[3072,768]{1,0:T(8,128)(2,1)}, s32[3072]{0:T(1024)S(1)}, bf16[3072,768]{1,0:T(8,128)(2,1)}) %tuple.72), branch_computations={%region_1.1_spmd, %region_2.4_spmd} | conditional | flops 227481632 | bytes 13120912 | solution.py:119
  319.9 19.4 %conditional.4 = (bf16[24,3072]{1,0:T(8,128)(2,1)S(1)}, bf16[24,768]{0,1:T(8,128)(2,1)S(1)}) conditional(s32[]{:T(128)} %convert_element_type.97, () %tuple.71, (bf16[24,3072]{1,0:T(8,128)(2,1)S(1)}, f32[1,3072]{1,0:T(1,128)S(1)}, bf16[3072,768]{1,0:T(8,128)(2,1)}, s32[3072]{0:T(1024)S(1)}, bf16[3072,768]{1,0:T(8,128)(2,1)}) %tuple.72), branch_computations={%region_1.1_spmd, %region_2.4_spmd} | conditional | flops 227481632 | bytes 13120912 | solution.py:119
  354.8 19.4 %conditional.4 = (bf16[24,3072]{1,0:T(8,128)(2,1)S(1)}, bf16[24,768]{0,1:T(8,128)(2,1)S(1)}) conditional(s32[]{:T(128)} %convert_element_type.97, () %tuple.71, (bf16[24,3072]{1,0:T(8,128)(2,1)S(1)}, f32[1,3072]{1,0:T(1,128)S(1)}, bf16[3072,768]{1,0:T(8,128)(2,1)}, s32[3072]{0:T(1024)S(1)}, bf16[3072,768]{1,0:T(8,128)(2,1)}) %tuple.72), branch_computations={%region_1.1_spmd, %region_2.4_spmd} | conditional | flops 227481632 | bytes 13120912 | solution.py:119
  389.7 19.4 %conditional.4 = (bf16[24,3072]{1,0:T(8,128)(2,1)S(1)}, bf16[24,768]{0,1:T(8,128)(2,1)S(1)}) conditional(s32[]{:T(128)} %convert_element_type.97, () %tuple.71, (bf16[24,3072]{1,0:T(8,128)(2,1)S(1)}, f32[1,3072]{1,0:T(1,128)S(1)}, bf16[3072,768]{1,0:T(8,128)(2,1)}, s32[3072]{0:T(1024)S(1)}, bf16[3072,768]{1,0:T(8,128)(2,1)}) %tuple.72), branch_computations={%region_1.1_spmd, %region_2.4_spmd} | conditional | flops 227481632 | bytes 13120912 | solution.py:119
  464.8 23.6 %collective-permute-start = (bf16[24,3072]{1,0:T(8,128)(2,1)S(1)}, bf16[24,3072]{1,0:T(8,128)(2,1)S(1)}, u32[]{:S(2)}, u32[]{:S(2)}) collective-permute-start(bf16[24,3072]{1,0:T(8,128)(2,1)S(1)} %get-tuple-element.514), channel_id=1, source_target_pairs={{0,32},{32,64},{64,96},{96,128},{128,160},{160,192},{192,224},{224... | collective-permute-start | bytes 442376 | tf_op jit(solution)/shard_map/while/body/eval_jaxpr/ppermute | solution.py:12
  553.8 19.5 %collective-permute-start = (bf16[24,3072]{1,0:T(8,128)(2,1)S(1)}, bf16[24,3072]{1,0:T(8,128)(2,1)S(1)}, u32[]{:S(2)}, u32[]{:S(2)}) collective-permute-start(bf16[24,3072]{1,0:T(8,128)(2,1)S(1)} %get-tuple-element.514), channel_id=1, source_target_pairs={{0,32},{32,64},{64,96},{96,128},{128,160},{160,192},{192,224},{224... | collective-permute-start | bytes 442376 | tf_op jit(solution)/shard_map/while/body/eval_jaxpr/ppermute | solution.py:12
  634.4 22.8 %collective-permute-start = (bf16[24,3072]{1,0:T(8,128)(2,1)S(1)}, bf16[24,3072]{1,0:T(8,128)(2,1)S(1)}, u32[]{:S(2)}, u32[]{:S(2)}) collective-permute-start(bf16[24,3072]{1,0:T(8,128)(2,1)S(1)} %get-tuple-element.514), channel_id=1, source_target_pairs={{0,32},{32,64},{64,96},{96,128},{128,160},{160,192},{192,224},{224... | collective-permute-start | bytes 442376 | tf_op jit(solution)/shard_map/while/body/eval_jaxpr/ppermute | solution.py:12
  700.8 798.9 %while.31 = (s32[]{:T(128)}, bf16[24,3072]{1,0:T(8,128)(2,1)S(1)}, bf16[6,24,768]{2,1,0:T(8,128)(2,1)S(1)}, s32[21]{0:T(128)S(1)}, s32[]{:T(128)}, /*index=5*/pr...) while((s32[]{:T(128)}, bf16[24,3072]{1,0:T(8,128)(2,1)S(1)}, ...), condition=%wide.region_11.13_spmd, body=%wide.region_6.12_spmd.sunk | while | flops 227942480 | bytes 15207745 | solution.py:153
  805.6 19.8 %collective-permute-done.1 = bf16[24,3072]{1,0:T(8,128)(2,1)S(1)} collective-permute-done((bf16[24,3072]{1,0:T(8,128)(2,1)S(1)}, bf16[24,3072]{1,0:T(8,128)(2,1)S(1)}, u32[]{:S(2)}, u32[]{:S(2)}) %collective-permute-start.1) | collective-permute-done | bytes 147488 | tf_op jit(solution)/shard_map/while/body/eval_jaxpr/ppermute | solution.py:12
  953.2 274.6 %collective-permute-done.1 = bf16[24,3072]{1,0:T(8,128)(2,1)S(1)} collective-permute-done((bf16[24,3072]{1,0:T(8,128)(2,1)S(1)}, bf16[24,3072]{1,0:T(8,128)(2,1)S(1)}, u32[]{:S(2)}, u32[]{:S(2)}) %collective-permute-start.1) | collective-permute-done | bytes 147488 | tf_op jit(solution)/shard_map/while/body/eval_jaxpr/ppermute | solution.py:12
  1229.9 20.4 %conditional.5 = (bf16[24,3072]{1,0:T(8,128)(2,1)S(1)}) conditional(s32[]{:T(128)} %convert_element_type.98, () %tuple.74, (bf16[24,3072]{1,0:T(8,128)(2,1)S(1)}, bf16[6,24,3072]{2,1,0:T(8,128)(2,1)S(1)}, s32[]{:T(128)}, bf16[3072,768]{1,0:T(8,128)(2,1)}, s32[3072]{0:T(1024)S(1)}, /*index=5*/bf16[3072,768]{1,0:T(8,128)(2,1)}, ...), branch_computations={%region_7.8_spmd, %region_8.11_spmd} | conditional | flops 227850304 | bytes 13990880 | solution.py:135
  1269.1 20.4 %conditional.5 = (bf16[24,3072]{1,0:T(8,128)(2,1)S(1)}) conditional(s32[]{:T(128)} %convert_element_type.98, () %tuple.74, (bf16[24,3072]{1,0:T(8,128)(2,1)S(1)}, bf16[6,24,3072]{2,1,0:T(8,128)(2,1)S(1)}, s32[]{:T(128)}, bf16[3072,768]{1,0:T(8,128)(2,1)}, s32[3072]{0:T(1024)S(1)}, /*index=5*/bf16[3072,768]{1,0:T(8,128)(2,1)}, ...), branch_computations={%region_7.8_spmd, %region_8.11_spmd} | conditional | flops 227850304 | bytes 13990880 | solution.py:135
  1312.6 20.4 %conditional.5 = (bf16[24,3072]{1,0:T(8,128)(2,1)S(1)}) conditional(s32[]{:T(128)} %convert_element_type.98, () %tuple.74, (bf16[24,3072]{1,0:T(8,128)(2,1)S(1)}, bf16[6,24,3072]{2,1,0:T(8,128)(2,1)S(1)}, s32[]{:T(128)}, bf16[3072,768]{1,0:T(8,128)(2,1)}, s32[3072]{0:T(1024)S(1)}, /*index=5*/bf16[3072,768]{1,0:T(8,128)(2,1)}, ...), branch_computations={%region_7.8_spmd, %region_8.11_spmd} | conditional | flops 227850304 | bytes 13990880 | solution.py:135
  1349.5 20.4 %conditional.5 = (bf16[24,3072]{1,0:T(8,128)(2,1)S(1)}) conditional(s32[]{:T(128)} %convert_element_type.98, () %tuple.74, (bf16[24,3072]{1,0:T(8,128)(2,1)S(1)}, bf16[6,24,3072]{2,1,0:T(8,128)(2,1)S(1)}, s32[]{:T(128)}, bf16[3072,768]{1,0:T(8,128)(2,1)}, s32[3072]{0:T(1024)S(1)}, /*index=5*/bf16[3072,768]{1,0:T(8,128)(2,1)}, ...), branch_computations={%region_7.8_spmd, %region_8.11_spmd} | conditional | flops 227850304 | bytes 13990880 | solution.py:135
  1385.7 20.4 %conditional.5 = (bf16[24,3072]{1,0:T(8,128)(2,1)S(1)}) conditional(s32[]{:T(128)} %convert_element_type.98, () %tuple.74, (bf16[24,3072]{1,0:T(8,128)(2,1)S(1)}, bf16[6,24,3072]{2,1,0:T(8,128)(2,1)S(1)}, s32[]{:T(128)}, bf16[3072,768]{1,0:T(8,128)(2,1)}, s32[3072]{0:T(1024)S(1)}, /*index=5*/bf16[3072,768]{1,0:T(8,128)(2,1)}, ...), branch_computations={%region_7.8_spmd, %region_8.11_spmd} | conditional | flops 227850304 | bytes 13990880 | solution.py:135
  1425.6 20.4 %conditional.5 = (bf16[24,3072]{1,0:T(8,128)(2,1)S(1)}) conditional(s32[]{:T(128)} %convert_element_type.98, () %tuple.74, (bf16[24,3072]{1,0:T(8,128)(2,1)S(1)}, bf16[6,24,3072]{2,1,0:T(8,128)(2,1)S(1)}, s32[]{:T(128)}, bf16[3072,768]{1,0:T(8,128)(2,1)}, s32[3072]{0:T(1024)S(1)}, /*index=5*/bf16[3072,768]{1,0:T(8,128)(2,1)}, ...), branch_computations={%region_7.8_spmd, %region_8.11_spmd} | conditional | flops 227850304 | bytes 13990880 | solution.py:135
  1459.1 23.2 %collective-permute-start.1 = (bf16[24,3072]{1,0:T(8,128)(2,1)S(1)}, bf16[24,3072]{1,0:T(8,128)(2,1)S(1)}, u32[]{:S(2)}, u32[]{:S(2)}) collective-permute-start(bf16[24,3072]{1,0:T(8,128)(2,1)S(1)} %get-tuple-element.635), channel_id=1, source_target_pairs={{32,0},{64,32},{96,64},{128,96},{160,128},{192,160},{224,192},{256... | collective-permute-start | bytes 442376 | tf_op jit(solution)/shard_map/while/body/eval_jaxpr/ppermute | solution.py:12
  1502.6 295.8 %all-reduce.2.cloned.1.call-done = bf16[768,768]{1,0:T(8,128)(2,1)} async-done(((bf16[768,768]{1,0:T(8,128)(2,1)}), bf16[768,768]{1,0:T(8,128)(2,1)}) %all-reduce.2.cloned.1.call-update) | async-done | bytes 1179664 | tf_op jit(solution)/shard_map/psum | solution.py:163
  (586 shorter events, 924.5 us)
Async XLA Ops:
  7.2 73.9 %all-gather.5.cloned.1.call-start = ((), (), s32[]{:S(2)}) async-start(), calls=%async_computation.1 | async-start | bytes 4866048 | tf_op jit(solution)/shard_map/all_gather | solution.py:82
  7.9 140.6 %all-gather.7.cloned.1.call-start = ((), (), s32[]{:S(2)}) async-start(), calls=%async_computation.2 | async-start | bytes 4866048 | tf_op jit(solution)/shard_map/all_gather | solution.py:83
  8.7 1789.7 %all-reduce.2.cloned.1.call-start = ((), (), s32[]{:S(2)}) async-start(), calls=%async_computation | async-start | bytes 2359296 | tf_op jit(solution)/shard_map/psum | solution.py:163
  170.5 41.5 %collective-permute-start = (bf16[24,3072]{1,0:T(8,128)(2,1)S(1)}, bf16[24,3072]{1,0:T(8,128)(2,1)S(1)}, u32[]{:S(2)}, u32[]{:S(2)}) collective-permute-start(bf16[24,3072]{1,0:T(8,128)(2,1)S(1)} %get-tuple-element.514), channel_id=1, source_target_pairs={{0,32},{32,64},{64,96},{96,128},{128,160},{160,192},{192,224},{224... | collective-permute-start | bytes 442376 | tf_op jit(solution)/shard_map/while/body/eval_jaxpr/ppermute | solution.py:12
  424.8 22.2 %collective-permute-start = (bf16[24,3072]{1,0:T(8,128)(2,1)S(1)}, bf16[24,3072]{1,0:T(8,128)(2,1)S(1)}, u32[]{:S(2)}, u32[]{:S(2)}) collective-permute-start(bf16[24,3072]{1,0:T(8,128)(2,1)S(1)} %get-tuple-element.514), channel_id=1, source_target_pairs={{0,32},{32,64},{64,96},{96,128},{128,160},{160,192},{192,224},{224... | collective-permute-start | bytes 442376 | tf_op jit(solution)/shard_map/while/body/eval_jaxpr/ppermute | solution.py:12
  464.8 27.0 %collective-permute-start = (bf16[24,3072]{1,0:T(8,128)(2,1)S(1)}, bf16[24,3072]{1,0:T(8,128)(2,1)S(1)}, u32[]{:S(2)}, u32[]{:S(2)}) collective-permute-start(bf16[24,3072]{1,0:T(8,128)(2,1)S(1)} %get-tuple-element.514), channel_id=1, source_target_pairs={{0,32},{32,64},{64,96},{96,128},{128,160},{160,192},{192,224},{224... | collective-permute-start | bytes 442376 | tf_op jit(solution)/shard_map/while/body/eval_jaxpr/ppermute | solution.py:12
  511.9 21.7 %collective-permute-start = (bf16[24,3072]{1,0:T(8,128)(2,1)S(1)}, bf16[24,3072]{1,0:T(8,128)(2,1)S(1)}, u32[]{:S(2)}, u32[]{:S(2)}) collective-permute-start(bf16[24,3072]{1,0:T(8,128)(2,1)S(1)} %get-tuple-element.514), channel_id=1, source_target_pairs={{0,32},{32,64},{64,96},{96,128},{128,160},{160,192},{192,224},{224... | collective-permute-start | bytes 442376 | tf_op jit(solution)/shard_map/while/body/eval_jaxpr/ppermute | solution.py:12
  553.8 22.8 %collective-permute-start = (bf16[24,3072]{1,0:T(8,128)(2,1)S(1)}, bf16[24,3072]{1,0:T(8,128)(2,1)S(1)}, u32[]{:S(2)}, u32[]{:S(2)}) collective-permute-start(bf16[24,3072]{1,0:T(8,128)(2,1)S(1)} %get-tuple-element.514), channel_id=1, source_target_pairs={{0,32},{32,64},{64,96},{96,128},{128,160},{160,192},{192,224},{224... | collective-permute-start | bytes 442376 | tf_op jit(solution)/shard_map/while/body/eval_jaxpr/ppermute | solution.py:12
  598.5 18.4 %collective-permute-start = (bf16[24,3072]{1,0:T(8,128)(2,1)S(1)}, bf16[24,3072]{1,0:T(8,128)(2,1)S(1)}, u32[]{:S(2)}, u32[]{:S(2)}) collective-permute-start(bf16[24,3072]{1,0:T(8,128)(2,1)S(1)} %get-tuple-element.514), channel_id=1, source_target_pairs={{0,32},{32,64},{64,96},{96,128},{128,160},{160,192},{192,224},{224... | collective-permute-start | bytes 442376 | tf_op jit(solution)/shard_map/while/body/eval_jaxpr/ppermute | solution.py:12
  634.4 26.2 %collective-permute-start = (bf16[24,3072]{1,0:T(8,128)(2,1)S(1)}, bf16[24,3072]{1,0:T(8,128)(2,1)S(1)}, u32[]{:S(2)}, u32[]{:S(2)}) collective-permute-start(bf16[24,3072]{1,0:T(8,128)(2,1)S(1)} %get-tuple-element.514), channel_id=1, source_target_pairs={{0,32},{32,64},{64,96},{96,128},{128,160},{160,192},{192,224},{224... | collective-permute-start | bytes 442376 | tf_op jit(solution)/shard_map/while/body/eval_jaxpr/ppermute | solution.py:12
  662.9 17.4 collective-permute-start
  682.7 18.1 %collective-permute-start = (bf16[24,3072]{1,0:T(8,128)(2,1)S(1)}, bf16[24,3072]{1,0:T(8,128)(2,1)S(1)}, u32[]{:S(2)}, u32[]{:S(2)}) collective-permute-start(bf16[24,3072]{1,0:T(8,128)(2,1)S(1)} %get-tuple-element.514), channel_id=1, source_target_pairs={{0,32},{32,64},{64,96},{96,128},{128,160},{160,192},{192,224},{224... | collective-permute-start | bytes 442376 | tf_op jit(solution)/shard_map/while/body/eval_jaxpr/ppermute | solution.py:12
  722.4 20.7 %collective-permute-start.1 = (bf16[24,3072]{1,0:T(8,128)(2,1)S(1)}, bf16[24,3072]{1,0:T(8,128)(2,1)S(1)}, u32[]{:S(2)}, u32[]{:S(2)}) collective-permute-start(bf16[24,3072]{1,0:T(8,128)(2,1)S(1)} %get-tuple-element.635), channel_id=1, source_target_pairs={{32,0},{64,32},{96,64},{128,96},{160,128},{192,160},{224,192},{256... | collective-permute-start | bytes 442376 | tf_op jit(solution)/shard_map/while/body/eval_jaxpr/ppermute | solution.py:12
  763.2 19.5 %collective-permute-start.1 = (bf16[24,3072]{1,0:T(8,128)(2,1)S(1)}, bf16[24,3072]{1,0:T(8,128)(2,1)S(1)}, u32[]{:S(2)}, u32[]{:S(2)}) collective-permute-start(bf16[24,3072]{1,0:T(8,128)(2,1)S(1)} %get-tuple-element.635), channel_id=1, source_target_pairs={{32,0},{64,32},{96,64},{128,96},{160,128},{192,160},{224,192},{256... | collective-permute-start | bytes 442376 | tf_op jit(solution)/shard_map/while/body/eval_jaxpr/ppermute | solution.py:12
  803.6 21.7 %collective-permute-start.1 = (bf16[24,3072]{1,0:T(8,128)(2,1)S(1)}, bf16[24,3072]{1,0:T(8,128)(2,1)S(1)}, u32[]{:S(2)}, u32[]{:S(2)}) collective-permute-start(bf16[24,3072]{1,0:T(8,128)(2,1)S(1)} %get-tuple-element.635), channel_id=1, source_target_pairs={{32,0},{64,32},{96,64},{128,96},{160,128},{192,160},{224,192},{256... | collective-permute-start | bytes 442376 | tf_op jit(solution)/shard_map/while/body/eval_jaxpr/ppermute | solution.py:12
  844.5 21.2 %collective-permute-start.1 = (bf16[24,3072]{1,0:T(8,128)(2,1)S(1)}, bf16[24,3072]{1,0:T(8,128)(2,1)S(1)}, u32[]{:S(2)}, u32[]{:S(2)}) collective-permute-start(bf16[24,3072]{1,0:T(8,128)(2,1)S(1)} %get-tuple-element.635), channel_id=1, source_target_pairs={{32,0},{64,32},{96,64},{128,96},{160,128},{192,160},{224,192},{256... | collective-permute-start | bytes 442376 | tf_op jit(solution)/shard_map/while/body/eval_jaxpr/ppermute | solution.py:12
  867.9 18.2 %collective-permute-start.1 = (bf16[24,3072]{1,0:T(8,128)(2,1)S(1)}, bf16[24,3072]{1,0:T(8,128)(2,1)S(1)}, u32[]{:S(2)}, u32[]{:S(2)}) collective-permute-start(bf16[24,3072]{1,0:T(8,128)(2,1)S(1)} %get-tuple-element.635), channel_id=1, source_target_pairs={{32,0},{64,32},{96,64},{128,96},{160,128},{192,160},{224,192},{256... | collective-permute-start | bytes 442376 | tf_op jit(solution)/shard_map/while/body/eval_jaxpr/ppermute | solution.py:12
  888.3 20.2 %collective-permute-start.1 = (bf16[24,3072]{1,0:T(8,128)(2,1)S(1)}, bf16[24,3072]{1,0:T(8,128)(2,1)S(1)}, u32[]{:S(2)}, u32[]{:S(2)}) collective-permute-start(bf16[24,3072]{1,0:T(8,128)(2,1)S(1)} %get-tuple-element.635), channel_id=1, source_target_pairs={{32,0},{64,32},{96,64},{128,96},{160,128},{192,160},{224,192},{256... | collective-permute-start | bytes 442376 | tf_op jit(solution)/shard_map/while/body/eval_jaxpr/ppermute | solution.py:12
  910.7 18.6 %collective-permute-start.1 = (bf16[24,3072]{1,0:T(8,128)(2,1)S(1)}, bf16[24,3072]{1,0:T(8,128)(2,1)S(1)}, u32[]{:S(2)}, u32[]{:S(2)}) collective-permute-start(bf16[24,3072]{1,0:T(8,128)(2,1)S(1)} %get-tuple-element.635), channel_id=1, source_target_pairs={{32,0},{64,32},{96,64},{128,96},{160,128},{192,160},{224,192},{256... | collective-permute-start | bytes 442376 | tf_op jit(solution)/shard_map/while/body/eval_jaxpr/ppermute | solution.py:12
  931.5 17.4 collective-permute-start.1
  951.2 276.5 %collective-permute-start.1 = (bf16[24,3072]{1,0:T(8,128)(2,1)S(1)}, bf16[24,3072]{1,0:T(8,128)(2,1)S(1)}, u32[]{:S(2)}, u32[]{:S(2)}) collective-permute-start(bf16[24,3072]{1,0:T(8,128)(2,1)S(1)} %get-tuple-element.635), channel_id=1, source_target_pairs={{32,0},{64,32},{96,64},{128,96},{160,128},{192,160},{224,192},{256... | collective-permute-start | bytes 442376 | tf_op jit(solution)/shard_map/while/body/eval_jaxpr/ppermute | solution.py:12
  1289.5 20.9 %collective-permute-start.1 = (bf16[24,3072]{1,0:T(8,128)(2,1)S(1)}, bf16[24,3072]{1,0:T(8,128)(2,1)S(1)}, u32[]{:S(2)}, u32[]{:S(2)}) collective-permute-start(bf16[24,3072]{1,0:T(8,128)(2,1)S(1)} %get-tuple-element.635), channel_id=1, source_target_pairs={{32,0},{64,32},{96,64},{128,96},{160,128},{192,160},{224,192},{256... | collective-permute-start | bytes 442376 | tf_op jit(solution)/shard_map/while/body/eval_jaxpr/ppermute | solution.py:12
  1406.1 17.3 collective-permute-start.1
  1459.1 25.9 %collective-permute-start.1 = (bf16[24,3072]{1,0:T(8,128)(2,1)S(1)}, bf16[24,3072]{1,0:T(8,128)(2,1)S(1)}, u32[]{:S(2)}, u32[]{:S(2)}) collective-permute-start(bf16[24,3072]{1,0:T(8,128)(2,1)S(1)} %get-tuple-element.635), channel_id=1, source_target_pairs={{32,0},{64,32},{96,64},{128,96},{160,128},{192,160},{224,192},{256... | collective-permute-start | bytes 442376 | tf_op jit(solution)/shard_map/while/body/eval_jaxpr/ppermute | solution.py:12
  (23 other events, 588.6 us)
Sparse Core Ops, SparseCore 0:
  10.1 70.8 all-gather.4
  83.2 65.3 all-gather.6
  1502.7 295.6 all-reduce.1
where the time goes:
time: 1810 us
  waiting for transfers between devices  1080 us (60%)
  starting transfers between devices  289 us (16%)
  local copies, waits for them, and re-layouts  199 us (11%)
  other arithmetic  110 us (6%)
  matrix products  84.7 us (5%)
  loops' own time  30.9 us (2%)
    ppermute x42, waiting for transfers between devices, shifted(): return lax.ppermute(array, axis, pairs)  655 us
    psum x1, waiting for transfers between devices, per_device(): left_total = lax.psum(left_term, 'dp').astype(jnp.float32)  296 us
    ppermute x42, starting transfers between devices, shifted(): return lax.ppermute(array, axis, pairs)  289 us
    all_gather x1, waiting for transfers between devices, per_device(): lax.all_gather(left_factor[0], 'dp', axis=0, tiled=True)  67.5 us
    all_gather x1, waiting for transfers between devices, per_device(): lax.all_gather(right_factor[0], 'dp', axis=0, tiled=True)  59.8 us
    gather x6, local copies, waits for them, and re-layouts, layer_forward(): permuted = jnp.take(mixed, shuffle, axis=1)  55 us
    gather x6, local copies, waits for them, and re-layouts, layer_backward(): before = jnp.take(through, inverse, axis=1)  55 us
    dynamic_update_slice x84, other arithmetic, store_slot(): lax.dynamic_update_index_in_dim(buffer, jnp.where(is_valid, new_value, ol...  51.3 us
  transfers between devices with their start and end apart: 45, of which 37 were waited for; matrix products, arithmetic and copies ran while one was open for 5% of the time, Pallas kernels for 0%

commit v1 on v0

--- a/solution.py
+++ b/solution.py
@@ -160,7 +160,7 @@
         left_rows, right_rows, (((0,), (0,)), ((), ())), preferred_element_type=jnp.float32
     )
     left_term = left_term.astype(jnp.bfloat16)
-    left_total = lax.psum(left_term, "dp").astype(jnp.float32)
+    left_total = jnp.sum(lax.all_gather(left_term, "dp"), axis=0).astype(jnp.float32)
     share_rows = block_size // lax.axis_size("dp")
     first_row = lax.axis_index("dp") * share_rows
     left_shard = lax.dynamic_slice_in_dim(left_total, first_row, share_rows, 0)

time: 1810 us -> 1750 us (0.967)
  the two profiles are of different devices: /device:TPU:8 before, /device:TPU:1 now
where the time goes in v1:
time: 1750 us
  waiting for transfers between devices  998 us (57%)
  starting transfers between devices  298 us (17%)
  local copies, waits for them, and re-layouts  199 us (11%)
  other arithmetic  122 us (7%)
  matrix products  84.7 us (5%)
  loops' own time  30.9 us (2%)
    ppermute x42, waiting for transfers between devices, shifted(): return lax.ppermute(array, axis, pairs)  614 us
    ppermute x42, starting transfers between devices, shifted(): return lax.ppermute(array, axis, pairs)  298 us
    all_gather x1, waiting for transfers between devices, per_device(): lax.all_gather(left_term, 'dp')  254 us
    all_gather x1, waiting for transfers between devices, per_device(): lax.all_gather(left_factor[0], 'dp', axis=0, tiled=True)  67.5 us
    all_gather x1, waiting for transfers between devices, per_device(): lax.all_gather(right_factor[0], 'dp', axis=0, tiled=True)  61.1 us
    gather x6, local copies, waits for them, and re-layouts, layer_backward(): before = jnp.take(through, inverse, axis=1)  55 us
    gather x6, local copies, waits for them, and re-layouts, layer_forward(): permuted = jnp.take(mixed, shuffle, axis=1)  55 us
    dynamic_update_slice x84, other arithmetic, store_slot(): lax.dynamic_update_index_in_dim(buffer, jnp.where(is_valid, new_value, ol...  51.3 us
  transfers between devices with their start and end apart: 45, of which 24 were waited for; matrix products, arithmetic and copies ran while one was open for 5% of the time, Pallas kernels for 0%

profile of v1, /device:TPU:1, one launch (start us, length us, event | category | flops | bytes accessed | tf_op | source)
XLA Modules:
  0.0 1746.1 jit_solution(14217181216083214808)
XLA Ops:
  21.3 61.1 %all-gather.7.cloned.1.call-done = bf16[1,3072,768]{2,1,0:T(8,128)(2,1)} async-done(((bf16[1,96,768]{2,1,0:T(8,128)(2,1)}), bf16[1,3072,768]{2,1,0:T(8,128)(2,1)}) %all-gather.7.cloned.1.call-update) | async-done | bytes 4718608 | tf_op jit(solution)/shard_map/all_gather | solution.py:82
  82.3 67.5 %all-gather.9.cloned.1.call-done = bf16[1,3072,768]{2,1,0:T(8,128)(2,1)} async-done(((bf16[1,96,768]{2,1,0:T(8,128)(2,1)}), bf16[1,3072,768]{2,1,0:T(8,128)(2,1)}) %all-gather.9.cloned.1.call-update) | async-done | bytes 4718608 | tf_op jit(solution)/shard_map/all_gather | solution.py:83
  152.1 506.0 %while.30 = (s32[]{:T(128)}, bf16[24,3072]{1,0:T(8,128)(2,1)S(1)}, bf16[6,24,3072]{2,1,0:T(8,128)(2,1)S(1)}, bf16[6,24,768]{1,2,0:T(8,128)(2,1)}, bf16[6,24,3072...) while((s32[]{:T(128)}, bf16[24,3072]{1,0:T(8,128)(2,1)S(1)}, ...), condition=%wide.region_4.6_spmd, body=%wide.region_0.5_spmd.sunk | while | flops 227721248 | bytes 15824611 | solution.py:146
  339.6 25.7 %collective-permute-start = (bf16[24,3072]{1,0:T(8,128)(2,1)S(1)}, bf16[24,3072]{1,0:T(8,128)(2,1)S(1)}, u32[]{:S(2)}, u32[]{:S(2)}) collective-permute-start(bf16[24,3072]{1,0:T(8,128)(2,1)S(1)} %get-tuple-element.514), channel_id=1, source_target_pairs={{0,32},{32,64},{64,96},{96,128},{128,160},{160,192},{192,224},{224... | collective-permute-start | bytes 442376 | tf_op jit(solution)/shard_map/while/body/eval_jaxpr/ppermute | solution.py:12
  383.4 26.6 %collective-permute-start = (bf16[24,3072]{1,0:T(8,128)(2,1)S(1)}, bf16[24,3072]{1,0:T(8,128)(2,1)S(1)}, u32[]{:S(2)}, u32[]{:S(2)}) collective-permute-start(bf16[24,3072]{1,0:T(8,128)(2,1)S(1)} %get-tuple-element.514), channel_id=1, source_target_pairs={{0,32},{32,64},{64,96},{96,128},{128,160},{160,192},{192,224},{224... | collective-permute-start | bytes 442376 | tf_op jit(solution)/shard_map/while/body/eval_jaxpr/ppermute | solution.py:12
  467.8 21.2 %collective-permute-start = (bf16[24,3072]{1,0:T(8,128)(2,1)S(1)}, bf16[24,3072]{1,0:T(8,128)(2,1)S(1)}, u32[]{:S(2)}, u32[]{:S(2)}) collective-permute-start(bf16[24,3072]{1,0:T(8,128)(2,1)S(1)} %get-tuple-element.514), channel_id=1, source_target_pairs={{0,32},{32,64},{64,96},{96,128},{128,160},{160,192},{192,224},{224... | collective-permute-start | bytes 442376 | tf_op jit(solution)/shard_map/while/body/eval_jaxpr/ppermute | solution.py:12
  507.7 21.3 %collective-permute-start = (bf16[24,3072]{1,0:T(8,128)(2,1)S(1)}, bf16[24,3072]{1,0:T(8,128)(2,1)S(1)}, u32[]{:S(2)}, u32[]{:S(2)}) collective-permute-start(bf16[24,3072]{1,0:T(8,128)(2,1)S(1)} %get-tuple-element.514), channel_id=1, source_target_pairs={{0,32},{32,64},{64,96},{96,128},{128,160},{160,192},{192,224},{224... | collective-permute-start | bytes 442376 | tf_op jit(solution)/shard_map/while/body/eval_jaxpr/ppermute | solution.py:12
  550.0 21.7 %collective-permute-start = (bf16[24,3072]{1,0:T(8,128)(2,1)S(1)}, bf16[24,3072]{1,0:T(8,128)(2,1)S(1)}, u32[]{:S(2)}, u32[]{:S(2)}) collective-permute-start(bf16[24,3072]{1,0:T(8,128)(2,1)S(1)} %get-tuple-element.514), channel_id=1, source_target_pairs={{0,32},{32,64},{64,96},{96,128},{128,160},{160,192},{192,224},{224... | collective-permute-start | bytes 442376 | tf_op jit(solution)/shard_map/while/body/eval_jaxpr/ppermute | solution.py:12
  592.5 22.7 %collective-permute-start = (bf16[24,3072]{1,0:T(8,128)(2,1)S(1)}, bf16[24,3072]{1,0:T(8,128)(2,1)S(1)}, u32[]{:S(2)}, u32[]{:S(2)}) collective-permute-start(bf16[24,3072]{1,0:T(8,128)(2,1)S(1)} %get-tuple-element.514), channel_id=1, source_target_pairs={{0,32},{32,64},{64,96},{96,128},{128,160},{160,192},{192,224},{224... | collective-permute-start | bytes 442376 | tf_op jit(solution)/shard_map/while/body/eval_jaxpr/ppermute | solution.py:12
  658.1 810.9 %while.31 = (s32[]{:T(128)}, bf16[24,3072]{1,0:T(8,128)(2,1)S(1)}, bf16[6,24,768]{2,1,0:T(8,128)(2,1)S(1)}, s32[21]{0:T(128)S(1)}, s32[]{:T(128)}, /*index=5*/pr...) while((s32[]{:T(128)}, bf16[24,3072]{1,0:T(8,128)(2,1)S(1)}, ...), condition=%wide.region_11.13_spmd, body=%wide.region_6.12_spmd.sunk | while | flops 227942480 | bytes 15207745 | solution.py:153
  675.2 25.0 %collective-permute-done.1 = bf16[24,3072]{1,0:T(8,128)(2,1)S(1)} collective-permute-done((bf16[24,3072]{1,0:T(8,128)(2,1)S(1)}, bf16[24,3072]{1,0:T(8,128)(2,1)S(1)}, u32[]{:S(2)}, u32[]{:S(2)}) %collective-permute-start.1) | collective-permute-done | bytes 147488 | tf_op jit(solution)/shard_map/while/body/eval_jaxpr/ppermute | solution.py:12
  757.9 20.4 %collective-permute-done.1 = bf16[24,3072]{1,0:T(8,128)(2,1)S(1)} collective-permute-done((bf16[24,3072]{1,0:T(8,128)(2,1)S(1)}, bf16[24,3072]{1,0:T(8,128)(2,1)S(1)}, u32[]{:S(2)}, u32[]{:S(2)}) %collective-permute-start.1) | collective-permute-done | bytes 147488 | tf_op jit(solution)/shard_map/while/body/eval_jaxpr/ppermute | solution.py:12
  796.6 22.4 %collective-permute-done.1 = bf16[24,3072]{1,0:T(8,128)(2,1)S(1)} collective-permute-done((bf16[24,3072]{1,0:T(8,128)(2,1)S(1)}, bf16[24,3072]{1,0:T(8,128)(2,1)S(1)}, u32[]{:S(2)}, u32[]{:S(2)}) %collective-permute-start.1) | collective-permute-done | bytes 147488 | tf_op jit(solution)/shard_map/while/body/eval_jaxpr/ppermute | solution.py:12
  837.7 21.7 %collective-permute-done.1 = bf16[24,3072]{1,0:T(8,128)(2,1)S(1)} collective-permute-done((bf16[24,3072]{1,0:T(8,128)(2,1)S(1)}, bf16[24,3072]{1,0:T(8,128)(2,1)S(1)}, u32[]{:S(2)}, u32[]{:S(2)}) %collective-permute-start.1) | collective-permute-done | bytes 147488 | tf_op jit(solution)/shard_map/while/body/eval_jaxpr/ppermute | solution.py:12
  877.8 25.5 %collective-permute-done.1 = bf16[24,3072]{1,0:T(8,128)(2,1)S(1)} collective-permute-done((bf16[24,3072]{1,0:T(8,128)(2,1)S(1)}, bf16[24,3072]{1,0:T(8,128)(2,1)S(1)}, u32[]{:S(2)}, u32[]{:S(2)}) %collective-permute-start.1) | collective-permute-done | bytes 147488 | tf_op jit(solution)/shard_map/while/body/eval_jaxpr/ppermute | solution.py:12
  919.4 29.0 %collective-permute-done.1 = bf16[24,3072]{1,0:T(8,128)(2,1)S(1)} collective-permute-done((bf16[24,3072]{1,0:T(8,128)(2,1)S(1)}, bf16[24,3072]{1,0:T(8,128)(2,1)S(1)}, u32[]{:S(2)}, u32[]{:S(2)}) %collective-permute-start.1) | collective-permute-done | bytes 147488 | tf_op jit(solution)/shard_map/while/body/eval_jaxpr/ppermute | solution.py:12
  951.9 304.7 %collective-permute-done.1 = bf16[24,3072]{1,0:T(8,128)(2,1)S(1)} collective-permute-done((bf16[24,3072]{1,0:T(8,128)(2,1)S(1)}, bf16[24,3072]{1,0:T(8,128)(2,1)S(1)}, u32[]{:S(2)}, u32[]{:S(2)}) %collective-permute-start.1) | collective-permute-done | bytes 147488 | tf_op jit(solution)/shard_map/while/body/eval_jaxpr/ppermute | solution.py:12
  1258.8 20.4 %conditional.5 = (bf16[24,3072]{1,0:T(8,128)(2,1)S(1)}) conditional(s32[]{:T(128)} %convert_element_type.100, () %tuple.74, (bf16[24,3072]{1,0:T(8,128)(2,1)S(1)}, bf16[6,24,3072]{2,1,0:T(8,128)(2,1)S(1)}, s32[]{:T(128)}, bf16[3072,768]{1,0:T(8,128)(2,1)}, s32[3072]{0:T(1024)S(1)}, /*index=5*/bf16[3072,768]{1,0:T(8,128)(2,1)}, ...), branch_computations={%region_7.8_spmd, %region_8.11_spmd} | conditional | flops 227850304 | bytes 13990880 | solution.py:135
  1296.3 20.4 %conditional.5 = (bf16[24,3072]{1,0:T(8,128)(2,1)S(1)}) conditional(s32[]{:T(128)} %convert_element_type.100, () %tuple.74, (bf16[24,3072]{1,0:T(8,128)(2,1)S(1)}, bf16[6,24,3072]{2,1,0:T(8,128)(2,1)S(1)}, s32[]{:T(128)}, bf16[3072,768]{1,0:T(8,128)(2,1)}, s32[3072]{0:T(1024)S(1)}, /*index=5*/bf16[3072,768]{1,0:T(8,128)(2,1)}, ...), branch_computations={%region_7.8_spmd, %region_8.11_spmd} | conditional | flops 227850304 | bytes 13990880 | solution.py:135
  1335.3 20.4 %conditional.5 = (bf16[24,3072]{1,0:T(8,128)(2,1)S(1)}) conditional(s32[]{:T(128)} %convert_element_type.100, () %tuple.74, (bf16[24,3072]{1,0:T(8,128)(2,1)S(1)}, bf16[6,24,3072]{2,1,0:T(8,128)(2,1)S(1)}, s32[]{:T(128)}, bf16[3072,768]{1,0:T(8,128)(2,1)}, s32[3072]{0:T(1024)S(1)}, /*index=5*/bf16[3072,768]{1,0:T(8,128)(2,1)}, ...), branch_computations={%region_7.8_spmd, %region_8.11_spmd} | conditional | flops 227850304 | bytes 13990880 | solution.py:135
  1372.1 20.4 %conditional.5 = (bf16[24,3072]{1,0:T(8,128)(2,1)S(1)}) conditional(s32[]{:T(128)} %convert_element_type.100, () %tuple.74, (bf16[24,3072]{1,0:T(8,128)(2,1)S(1)}, bf16[6,24,3072]{2,1,0:T(8,128)(2,1)S(1)}, s32[]{:T(128)}, bf16[3072,768]{1,0:T(8,128)(2,1)}, s32[3072]{0:T(1024)S(1)}, /*index=5*/bf16[3072,768]{1,0:T(8,128)(2,1)}, ...), branch_computations={%region_7.8_spmd, %region_8.11_spmd} | conditional | flops 227850304 | bytes 13990880 | solution.py:135
  1405.4 20.4 %conditional.5 = (bf16[24,3072]{1,0:T(8,128)(2,1)S(1)}) conditional(s32[]{:T(128)} %convert_element_type.100, () %tuple.74, (bf16[24,3072]{1,0:T(8,128)(2,1)S(1)}, bf16[6,24,3072]{2,1,0:T(8,128)(2,1)S(1)}, s32[]{:T(128)}, bf16[3072,768]{1,0:T(8,128)(2,1)}, s32[3072]{0:T(1024)S(1)}, /*index=5*/bf16[3072,768]{1,0:T(8,128)(2,1)}, ...), branch_computations={%region_7.8_spmd, %region_8.11_spmd} | conditional | flops 227850304 | bytes 13990880 | solution.py:135
  1438.7 20.4 %conditional.5 = (bf16[24,3072]{1,0:T(8,128)(2,1)S(1)}) conditional(s32[]{:T(128)} %convert_element_type.100, () %tuple.74, (bf16[24,3072]{1,0:T(8,128)(2,1)S(1)}, bf16[6,24,3072]{2,1,0:T(8,128)(2,1)S(1)}, s32[]{:T(128)}, bf16[3072,768]{1,0:T(8,128)(2,1)}, s32[3072]{0:T(1024)S(1)}, /*index=5*/bf16[3072,768]{1,0:T(8,128)(2,1)}, ...), branch_computations={%region_7.8_spmd, %region_8.11_spmd} | conditional | flops 227850304 | bytes 13990880 | solution.py:135
  1472.0 254.0 %all-gather.11.cloned.1.call-done = bf16[24576,768]{1,0:T(8,128)(2,1)} async-done(((bf16[768,768]{1,0:T(8,128)(2,1)}), bf16[24576,768]{1,0:T(8,128)(2,1)}) %all-gather.11.cloned.1.call-update) | async-done | bytes 37748752 | tf_op jit(solution)/shard_map/all_gather | solution.py:163
  (587 shorter events, 848.6 us)
Async XLA Ops:
  7.2 75.2 %all-gather.7.cloned.1.call-start = ((), (), s32[]{:S(2)}) async-start(), calls=%async_computation | async-start | bytes 4866048 | tf_op jit(solution)/shard_map/all_gather | solution.py:82
  7.9 141.9 %all-gather.9.cloned.1.call-start = ((), (), s32[]{:S(2)}) async-start(), calls=%async_computation.1 | async-start | bytes 4866048 | tf_op jit(solution)/shard_map/all_gather | solution.py:83
  8.7 1717.3 %all-gather.11.cloned.1.call-start = ((), (), s32[]{:S(2)}) async-start(), calls=%async_computation.2 | async-start | bytes 38928384 | tf_op jit(solution)/shard_map/all_gather | solution.py:163
  339.6 29.1 %collective-permute-start = (bf16[24,3072]{1,0:T(8,128)(2,1)S(1)}, bf16[24,3072]{1,0:T(8,128)(2,1)S(1)}, u32[]{:S(2)}, u32[]{:S(2)}) collective-permute-start(bf16[24,3072]{1,0:T(8,128)(2,1)S(1)} %get-tuple-element.514), channel_id=1, source_target_pairs={{0,32},{32,64},{64,96},{96,128},{128,160},{160,192},{192,224},{224... | collective-permute-start | bytes 442376 | tf_op jit(solution)/shard_map/while/body/eval_jaxpr/ppermute | solution.py:12
  383.4 30.0 %collective-permute-start = (bf16[24,3072]{1,0:T(8,128)(2,1)S(1)}, bf16[24,3072]{1,0:T(8,128)(2,1)S(1)}, u32[]{:S(2)}, u32[]{:S(2)}) collective-permute-start(bf16[24,3072]{1,0:T(8,128)(2,1)S(1)} %get-tuple-element.514), channel_id=1, source_target_pairs={{0,32},{32,64},{64,96},{96,128},{128,160},{160,192},{192,224},{224... | collective-permute-start | bytes 442376 | tf_op jit(solution)/shard_map/while/body/eval_jaxpr/ppermute | solution.py:12
  428.8 23.6 %collective-permute-start = (bf16[24,3072]{1,0:T(8,128)(2,1)S(1)}, bf16[24,3072]{1,0:T(8,128)(2,1)S(1)}, u32[]{:S(2)}, u32[]{:S(2)}) collective-permute-start(bf16[24,3072]{1,0:T(8,128)(2,1)S(1)} %get-tuple-element.514), channel_id=1, source_target_pairs={{0,32},{32,64},{64,96},{96,128},{128,160},{160,192},{192,224},{224... | collective-permute-start | bytes 442376 | tf_op jit(solution)/shard_map/while/body/eval_jaxpr/ppermute | solution.py:12
  467.8 24.5 %collective-permute-start = (bf16[24,3072]{1,0:T(8,128)(2,1)S(1)}, bf16[24,3072]{1,0:T(8,128)(2,1)S(1)}, u32[]{:S(2)}, u32[]{:S(2)}) collective-permute-start(bf16[24,3072]{1,0:T(8,128)(2,1)S(1)} %get-tuple-element.514), channel_id=1, source_target_pairs={{0,32},{32,64},{64,96},{96,128},{128,160},{160,192},{192,224},{224... | collective-permute-start | bytes 442376 | tf_op jit(solution)/shard_map/while/body/eval_jaxpr/ppermute | solution.py:12
  507.7 24.6 %collective-permute-start = (bf16[24,3072]{1,0:T(8,128)(2,1)S(1)}, bf16[24,3072]{1,0:T(8,128)(2,1)S(1)}, u32[]{:S(2)}, u32[]{:S(2)}) collective-permute-start(bf16[24,3072]{1,0:T(8,128)(2,1)S(1)} %get-tuple-element.514), channel_id=1, source_target_pairs={{0,32},{32,64},{64,96},{96,128},{128,160},{160,192},{192,224},{224... | collective-permute-start | bytes 442376 | tf_op jit(solution)/shard_map/while/body/eval_jaxpr/ppermute | solution.py:12
  550.0 25.0 %collective-permute-start = (bf16[24,3072]{1,0:T(8,128)(2,1)S(1)}, bf16[24,3072]{1,0:T(8,128)(2,1)S(1)}, u32[]{:S(2)}, u32[]{:S(2)}) collective-permute-start(bf16[24,3072]{1,0:T(8,128)(2,1)S(1)} %get-tuple-element.514), channel_id=1, source_target_pairs={{0,32},{32,64},{64,96},{96,128},{128,160},{160,192},{192,224},{224... | collective-permute-start | bytes 442376 | tf_op jit(solution)/shard_map/while/body/eval_jaxpr/ppermute | solution.py:12
  592.5 26.0 %collective-permute-start = (bf16[24,3072]{1,0:T(8,128)(2,1)S(1)}, bf16[24,3072]{1,0:T(8,128)(2,1)S(1)}, u32[]{:S(2)}, u32[]{:S(2)}) collective-permute-start(bf16[24,3072]{1,0:T(8,128)(2,1)S(1)} %get-tuple-element.514), channel_id=1, source_target_pairs={{0,32},{32,64},{64,96},{96,128},{128,160},{160,192},{192,224},{224... | collective-permute-start | bytes 442376 | tf_op jit(solution)/shard_map/while/body/eval_jaxpr/ppermute | solution.py:12
  635.4 22.7 %collective-permute-start = (bf16[24,3072]{1,0:T(8,128)(2,1)S(1)}, bf16[24,3072]{1,0:T(8,128)(2,1)S(1)}, u32[]{:S(2)}, u32[]{:S(2)}) collective-permute-start(bf16[24,3072]{1,0:T(8,128)(2,1)S(1)} %get-tuple-element.514), channel_id=1, source_target_pairs={{0,32},{32,64},{64,96},{96,128},{128,160},{160,192},{192,224},{224... | collective-permute-start | bytes 442376 | tf_op jit(solution)/shard_map/while/body/eval_jaxpr/ppermute | solution.py:12
  673.9 26.4 %collective-permute-start.1 = (bf16[24,3072]{1,0:T(8,128)(2,1)S(1)}, bf16[24,3072]{1,0:T(8,128)(2,1)S(1)}, u32[]{:S(2)}, u32[]{:S(2)}) collective-permute-start(bf16[24,3072]{1,0:T(8,128)(2,1)S(1)} %get-tuple-element.635), channel_id=1, source_target_pairs={{32,0},{64,32},{96,64},{128,96},{160,128},{192,160},{224,192},{256... | collective-permute-start | bytes 442376 | tf_op jit(solution)/shard_map/while/body/eval_jaxpr/ppermute | solution.py:12
  702.4 15.5 collective-permute-start.1
  720.2 17.8 %collective-permute-start.1 = (bf16[24,3072]{1,0:T(8,128)(2,1)S(1)}, bf16[24,3072]{1,0:T(8,128)(2,1)S(1)}, u32[]{:S(2)}, u32[]{:S(2)}) collective-permute-start(bf16[24,3072]{1,0:T(8,128)(2,1)S(1)} %get-tuple-element.635), channel_id=1, source_target_pairs={{32,0},{64,32},{96,64},{128,96},{160,128},{192,160},{224,192},{256... | collective-permute-start | bytes 442376 | tf_op jit(solution)/shard_map/while/body/eval_jaxpr/ppermute | solution.py:12
  740.2 14.2 collective-permute-start.1
  756.6 21.7 %collective-permute-start.1 = (bf16[24,3072]{1,0:T(8,128)(2,1)S(1)}, bf16[24,3072]{1,0:T(8,128)(2,1)S(1)}, u32[]{:S(2)}, u32[]{:S(2)}) collective-permute-start(bf16[24,3072]{1,0:T(8,128)(2,1)S(1)} %get-tuple-element.635), channel_id=1, source_target_pairs={{32,0},{64,32},{96,64},{128,96},{160,128},{192,160},{224,192},{256... | collective-permute-start | bytes 442376 | tf_op jit(solution)/shard_map/while/body/eval_jaxpr/ppermute | solution.py:12
  795.3 23.8 %collective-permute-start.1 = (bf16[24,3072]{1,0:T(8,128)(2,1)S(1)}, bf16[24,3072]{1,0:T(8,128)(2,1)S(1)}, u32[]{:S(2)}, u32[]{:S(2)}) collective-permute-start(bf16[24,3072]{1,0:T(8,128)(2,1)S(1)} %get-tuple-element.635), channel_id=1, source_target_pairs={{32,0},{64,32},{96,64},{128,96},{160,128},{192,160},{224,192},{256... | collective-permute-start | bytes 442376 | tf_op jit(solution)/shard_map/while/body/eval_jaxpr/ppermute | solution.py:12
  836.4 23.1 %collective-permute-start.1 = (bf16[24,3072]{1,0:T(8,128)(2,1)S(1)}, bf16[24,3072]{1,0:T(8,128)(2,1)S(1)}, u32[]{:S(2)}, u32[]{:S(2)}) collective-permute-start(bf16[24,3072]{1,0:T(8,128)(2,1)S(1)} %get-tuple-element.635), channel_id=1, source_target_pairs={{32,0},{64,32},{96,64},{128,96},{160,128},{192,160},{224,192},{256... | collective-permute-start | bytes 442376 | tf_op jit(solution)/shard_map/while/body/eval_jaxpr/ppermute | solution.py:12
  876.4 26.9 %collective-permute-start.1 = (bf16[24,3072]{1,0:T(8,128)(2,1)S(1)}, bf16[24,3072]{1,0:T(8,128)(2,1)S(1)}, u32[]{:S(2)}, u32[]{:S(2)}) collective-permute-start(bf16[24,3072]{1,0:T(8,128)(2,1)S(1)} %get-tuple-element.635), channel_id=1, source_target_pairs={{32,0},{64,32},{96,64},{128,96},{160,128},{192,160},{224,192},{256... | collective-permute-start | bytes 442376 | tf_op jit(solution)/shard_map/while/body/eval_jaxpr/ppermute | solution.py:12
  918.0 30.3 %collective-permute-start.1 = (bf16[24,3072]{1,0:T(8,128)(2,1)S(1)}, bf16[24,3072]{1,0:T(8,128)(2,1)S(1)}, u32[]{:S(2)}, u32[]{:S(2)}) collective-permute-start(bf16[24,3072]{1,0:T(8,128)(2,1)S(1)} %get-tuple-element.635), channel_id=1, source_target_pairs={{32,0},{64,32},{96,64},{128,96},{160,128},{192,160},{224,192},{256... | collective-permute-start | bytes 442376 | tf_op jit(solution)/shard_map/while/body/eval_jaxpr/ppermute | solution.py:12
  950.6 306.0 %collective-permute-start.1 = (bf16[24,3072]{1,0:T(8,128)(2,1)S(1)}, bf16[24,3072]{1,0:T(8,128)(2,1)S(1)}, u32[]{:S(2)}, u32[]{:S(2)}) collective-permute-start(bf16[24,3072]{1,0:T(8,128)(2,1)S(1)} %get-tuple-element.635), channel_id=1, source_target_pairs={{32,0},{64,32},{96,64},{128,96},{160,128},{192,160},{224,192},{256... | collective-permute-start | bytes 442376 | tf_op jit(solution)/shard_map/while/body/eval_jaxpr/ppermute | solution.py:12
  1279.2 14.8 collective-permute-start.1
  1316.7 16.4 collective-permute-start.1
  1355.7 14.2 collective-permute-start.1
  (23 other events, 516.1 us)
Sparse Core Ops, SparseCore 0:
  10.1 72.1 all-gather.6
  84.5 65.2 all-gather.8
  1472.1 253.8 all-gather.10
